TPU v7x, 32 devices: a whole 2x2x4 slice. The times are simulated.
32 devices in a mesh: dp: 2 (over core), expert: 4 (over y, x), mp: 4 (over z).
Axes of the slice: x: 2, y: 2, z: 4, core: 2. Of those that a mesh axis runs over, the one named last changes fastest.
Arguments:
- tokens: bfloat16 [512, 3072], P(('dp', 'expert')), may hold values from -6 to 6
- w_router: float32 [3072, 4], replicated, may hold values from -0.109375 to 0.109375
- expert_ids: int32 [512, 2], P(('dp', 'expert')), may hold values from 0 to 3, all different within a row; in each aligned block of 64 rows (0 to 63, 64 to 127, ...) at most 64 rows name the same one
- partner: int32 [4], replicated, may hold values from 0 to 3, as said below
- gate_weight: bfloat16 [4, 3072, 8192], P('expert', None, ('dp', 'mp')), may hold values from -0.109375 to 0.109375
- up_weight: bfloat16 [4, 3072, 8192], P('expert', None, ('dp', 'mp')), may hold values from -0.109375 to 0.109375
- down_weight: bfloat16 [4, 8192, 3072], P('expert', ('dp', 'mp')), may hold values from -0.0625 to 0.0625
- grad_out: bfloat16 [512, 3072], P(('dp', 'expert')), may hold values from -1.5 to 1.5
Outputs:
- mixed: bfloat16 [512, 3072], P(('dp', 'expert'))
- grad_tokens: bfloat16 [512, 3072], P(('dp', 'expert'))
- grad_router: float32 [3072, 4], replicated
- grad_gate: bfloat16 [4, 3072, 8192], P('expert', None, ('dp', 'mp'))
- grad_up: bfloat16 [4, 3072, 8192], P('expert', None, ('dp', 'mp'))
- grad_down: bfloat16 [4, 8192, 3072], P('expert', ('dp', 'mp'))
Inputs may be any that keep to these rules, and one draw needn't show every extreme that they name: `expert_ids`: each token names two different experts. Within each aligned block of 64 tokens no expert is named by more than 64 tokens, and in every draw some block names some expert exactly 64 times. A matching of the experts: partner[partner[e]] = e and partner[e] != e for every expert e.
All inputs are finite; a program needn't handle non-finite values.
Results may differ from a plain program's by a relative error of at most 0.019.
Values may be sent and summed in bfloat16 or wider, within the bound.
No kernel may reach another device: no remote copies, remote signals or barrier semaphores. Data moves between devices by JAX's collectives and lax.ppermute only.
A program may use at most 128 MiB of HBM per device.

v0:
```python
import jax
import jax.numpy as jnp
from jax import lax
from jax.sharding import PartitionSpec as P

exact_mode = lax.Precision.HIGHEST


def local(tokens, w_router, expert_ids, partner, gate_weight, up_weight, down_weight, grad_out):
    tok_rows, features = tokens.shape
    experts = w_router.shape[1]
    hid_part = gate_weight.shape[2]
    dp_count = lax.axis_size("dp")
    exp_count = lax.axis_size("expert")
    slot_count = min(tok_rows, 4 * tok_rows // experts)
    keep_count = 3 * slot_count // 4
    slot_total = experts * slot_count
    block_rows = exp_count * slot_count
    floats = tokens.astype(jnp.float32)
    logits = jnp.dot(floats, w_router, precision=exact_mode)
    chosen = (expert_ids[:, :, None] == lax.iota(jnp.int32, experts)[None, None, :]).astype(
        jnp.int32
    )
    chosen_float = chosen.astype(jnp.float32)
    picked = jnp.sum(logits[:, None, :] * chosen_float, axis=2)
    share_one = jax.nn.sigmoid(picked[:, 0] - picked[:, 1])
    shares = jnp.stack([share_one, 1.0 - share_one], axis=1)
    flat_choice = chosen.reshape(2 * tok_rows, experts)
    earlier = jnp.cumsum(flat_choice, axis=0) - flat_choice
    arrival = jnp.sum(earlier * flat_choice, axis=1).reshape(tok_rows, 2)
    partner_of = jnp.sum(chosen * partner[None, None, :], axis=2)
    target = jnp.where(arrival < keep_count, expert_ids, partner_of)
    slot_index = target * slot_count + arrival
    placing = (slot_index[:, :, None] == lax.iota(jnp.int32, slot_total)[None, None, :]).astype(
        jnp.bfloat16
    )
    send_tokens = jnp.einsum("tks,td->sd", placing, tokens, preferred_element_type=jnp.float32)
    send_tokens = send_tokens.astype(jnp.bfloat16).reshape(experts, slot_count, features)
    scaled = (shares[:, :, None] * grad_out.astype(jnp.float32)[:, None, :]).astype(jnp.bfloat16)
    send_cot = jnp.einsum("tks,tkd->sd", placing, scaled, preferred_element_type=jnp.float32)
    send_cot = send_cot.astype(jnp.bfloat16).reshape(experts, slot_count, features)

    def spread(buffer):
        arrived = lax.all_to_all(buffer, "expert", split_axis=0, concat_axis=0, tiled=True)
        return lax.all_gather(arrived, "dp", axis=0, tiled=True)

    rows_in = spread(send_tokens).reshape(-1, features)
    pieces = 1

    def combine(partial_value):
        summed = lax.psum(
            partial_value.reshape(dp_count, block_rows, features).astype(jnp.bfloat16), ("dp", "mp")
        ).astype(jnp.float32)
        own_rows = lax.dynamic_index_in_dim(summed, lax.axis_index("dp"), 0, keepdims=False)
        own_rows = own_rows.astype(jnp.bfloat16).reshape(exp_count, slot_count, features)
        restored = lax.all_to_all(own_rows, "expert", split_axis=0, concat_axis=0, tiled=True)
        return restored.reshape(slot_total, features)

    w_gate = gate_weight[0]
    w_up = up_weight[0]
    w_down = down_weight[0]
    pre_gate = jnp.dot(rows_in, w_gate, preferred_element_type=jnp.float32)
    pre_up = jnp.dot(rows_in, w_up, preferred_element_type=jnp.float32)
    sigmoid_gate = jax.nn.sigmoid(pre_gate)
    swished = pre_gate * sigmoid_gate
    hidden = (swished * pre_up).astype(jnp.bfloat16)
    down_split = w_down.reshape(hid_part, pieces, features // pieces)
    forward_terms = jnp.einsum(
        "prf,fqd->pqrd",
        hidden.reshape(dp_count, block_rows, hid_part),
        down_split,
        preferred_element_type=jnp.float32,
    )
    expert_out = combine(forward_terms)
    back_rows = jnp.einsum("tks,sd->tkd", placing, expert_out, preferred_element_type=jnp.float32)
    mixed = (shares[:, 0, None] * back_rows[:, 0] + shares[:, 1, None] * back_rows[:, 1]).astype(
        jnp.bfloat16
    )
    falling = grad_out.astype(jnp.float32)
    dshare = jnp.sum(falling[:, None, :] * back_rows, axis=2)
    dlogit = shares[:, 0] * shares[:, 1] * (dshare[:, 0] - dshare[:, 1])
    grad_logits = (chosen_float[:, 0] - chosen_float[:, 1]) * dlogit[:, None]
    router_term = lax.dot_general(
        floats, grad_logits, (((0,), (0,)), ((), ())), precision=exact_mode
    )
    grad_router = lax.psum(router_term.astype(jnp.bfloat16), ("dp", "expert")).astype(jnp.float32)
    router_back = jnp.dot(grad_logits, w_router.T, precision=exact_mode)
    cot_in = spread(send_cot).reshape(-1, features)
    dhidden = jnp.einsum("rd,fd->rf", cot_in, w_down, preferred_element_type=jnp.float32)
    up_grad = (dhidden * swished).astype(jnp.bfloat16)
    gate_grad = (dhidden * pre_up * sigmoid_gate * (1.0 + pre_gate * (1.0 - sigmoid_gate))).astype(
        jnp.bfloat16
    )
    grad_down = jnp.einsum("rf,rd->fd", hidden, cot_in, preferred_element_type=jnp.float32).astype(
        jnp.bfloat16
    )[None]
    grad_gate = jnp.einsum(
        "rd,rf->df", rows_in, gate_grad, preferred_element_type=jnp.float32
    ).astype(jnp.bfloat16)[None]
    grad_up = jnp.einsum("rd,rf->df", rows_in, up_grad, preferred_element_type=jnp.float32).astype(
        jnp.bfloat16
    )[None]
    gate_split = w_gate.reshape(pieces, features // pieces, hid_part)
    up_split = w_up.reshape(pieces, features // pieces, hid_part)
    backward_terms = jnp.einsum(
        "prf,qdf->pqrd",
        gate_grad.reshape(dp_count, block_rows, hid_part),
        gate_split,
        preferred_element_type=jnp.float32,
    )
    backward_terms = backward_terms + jnp.einsum(
        "prf,qdf->pqrd",
        up_grad.reshape(dp_count, block_rows, hid_part),
        up_split,
        preferred_element_type=jnp.float32,
    )
    row_grads = combine(backward_terms)
    grad_rows = jnp.einsum("tks,sd->tkd", placing, row_grads, preferred_element_type=jnp.float32)
    grad_tokens = (router_back + grad_rows[:, 0] + grad_rows[:, 1]).astype(jnp.bfloat16)
    return (mixed, grad_tokens, grad_router, grad_gate, grad_up, grad_down)


def solution(mesh):
    in_specs = (
        P(("dp", "expert"), None),
        P(),
        P(("dp", "expert"), None),
        P(),
        P("expert", None, ("dp", "mp")),
        P("expert", None, ("dp", "mp")),
        P("expert", ("dp", "mp"), None),
        P(("dp", "expert"), None),
    )
    out_specs = (
        P(("dp", "expert"), None),
        P(("dp", "expert"), None),
        P(),
        P("expert", None, ("dp", "mp")),
        P("expert", None, ("dp", "mp")),
        P("expert", ("dp", "mp"), None),
    )
    return jax.shard_map(local, mesh=mesh, in_specs=in_specs, out_specs=out_specs, check_vma=False)
```

profile of v0, /device:TPU:1, one launch (start us, length us, event | category | flops | bytes accessed | tf_op | source)
XLA Modules:
  0.0 329.8 jit_solution(508223752091180420)
XLA Ops:
  7.2 0.0 copy-start
  7.2 0.0 all-gather.5.cloned.1.call-start
  7.2 0.8 copy.29
  8.0 0.1 copy-done
  8.2 1.2 fusion.42
  9.4 0.7 multiply_reduce_fusion.1
  10.1 0.1 eq.38
  10.3 0.1 fusion.34
  10.4 0.2 reduce_window_sum.11
  10.5 0.2 select_reduce_fusion
  10.7 0.1 reshape.71
  10.9 0.1 copy.30
  10.9 0.8 select_reduce_fusion.1
  11.7 1.0 convert_element_type.104
  12.8 0.7 fusion.38
  13.5 0.7 fusion.17
  14.2 22.7 %all_to_all.20 = bf16[4,64,3072]{2,1,0:T(8,128)(2,1)} all-to-all(bf16[4,64,3072]{2,1,0:T(8,128)(2,1)S(1)} %bitcast.108), channel_id=1, replica_groups=mesh['dp'=2,'expert'=4,'mp'=4] {'expert'}, dimensions={0} | all-to-all | bytes 3145728 | tf_op jit(solution)/shard_map/all_to_all | solution.py:44
  36.8 0.0 all-gather.5.cloned.1.call-update
  36.9 0.0 all-gather.3.cloned.1.call-start
  36.9 0.1 convert_reduce_fusion
  37.0 0.6 fusion.43
  37.6 20.3 %all_to_all.21 = bf16[4,64,3072]{2,1,0:T(8,128)(2,1)} all-to-all(bf16[4,64,3072]{2,1,0:T(8,128)(2,1)S(1)} %bitcast.105), channel_id=1, replica_groups=mesh['dp'=2,'expert'=4,'mp'=4] {'expert'}, dimensions={0} | all-to-all | bytes 3145728 | tf_op jit(solution)/shard_map/all_to_all | solution.py:44
  57.9 0.0 all-gather.3.cloned.1.call-update
  57.9 0.0 all-reduce.3.cloned.1.call-start
  58.0 0.0 all-gather.5.cloned.1.call-done
  58.0 6.5 %fusion.6 = f32[512,1024]{1,0:T(8,128)S(1)} fusion(bf16[512,3072]{1,0:T(8,128)(2,1)} %bitcast.120, bf16[1,1024,3072]{2,1,0:T(8,128)(2,1)} %param.14), kind=kOutput, calls=%fused_computation.6 | convolution fusion | flops 3221225472 | bytes 11534336 | tf_op jit(solution)/shard_map/rd,fd->rf/dot_general | solution.py:89
  64.6 8.7 %all-gather.3.cloned.1.call-done = bf16[8,64,3072]{2,1,0:T(8,128)(2,1)} async-done(((bf16[4,64,3072]{2,1,0:T(8,128)(2,1)}), bf16[8,64,3072]{2,1,0:T(8,128)(2,1)}) %all-gather.3.cloned.1.call-update) | async-done | bytes 3145744 | tf_op jit(solution)/shard_map/all_gather | solution.py:45
  73.3 6.6 %fusion.8 = f32[512,1024]{1,0:T(8,128)S(1)} fusion(bf16[512,3072]{1,0:T(8,128)(2,1)} %bitcast.116, bf16[1,3072,1024]{2,1,0:T(8,128)(2,1)} %param.13), kind=kOutput, calls=%fused_computation.8 | convolution fusion | flops 3221225472 | bytes 11534336 | tf_op jit(solution)/shard_map/dot_general | solution.py:63
  79.9 0.0 copy-done.5
  79.9 0.0 slice-start.1
  79.9 0.0 slice-start.3
  79.9 0.0 slice-start.4
  79.9 7.3 %multiply_convert_fusion.1 = (bf16[512,1024]{1,0:T(8,128)(2,1)S(1)}, bf16[512,1024]{1,0:T(8,128)(2,1)S(1)}, bf16[512,1024]{1,0:T(8,128)(2,1)S(1)}) fusion(f32[512,1024]{1,0:T(8,128)S(1)} %fusion.6, f32[512,1024]{1,0:T(8,128)S(1)} %fusion.8, bf16[512,3072]{1,0:T(8,128)(2,1)S(1)} %bitcast.118, bf16[1,3072,1024]{2,1,0:T(8,128)(2,1)} %param.12), kind=kOutput, calls=%fused_computation.28 | convolution fusion | flops 3229089792 | bytes 16777216 | tf_op jit(solution)/shard_map/dot_general | solution.py:62
  87.2 0.0 copy-start.9
  87.2 0.0 copy-start.10
  87.2 0.0 copy-start.7
  87.3 0.0 slice-done
  87.3 0.0 slice-done.1
  87.3 0.0 slice-start.5
  87.3 5.4 %fusion = f32[2,256,3072]{2,1,0:T(8,128)} fusion(bf16[2,256,1024]{2,1,0:T(8,128)(2,1)S(1)} %bitcast.123, bf16[1,3072,1024]{2,1,0:T(8,128)(2,1)S(1)} %bitcast.111), kind=kOutput, calls=%fused_computation | convolution fusion | flops 3221225472 | bytes 13631488 | tf_op jit(solution)/shard_map/prf,qdf->pqrd/dot_general | solution.py:111
  92.7 0.0 copy-done.9
  92.7 0.0 slice-done.3
  92.7 4.8 %fusion.14 = bf16[2,256,3072]{2,1,0:T(8,128)(2,1)} fusion(bf16[2,256,1024]{2,1,0:T(8,128)(2,1)S(1)} %bitcast.124, bf16[1,1024,3072]{2,1,0:T(8,128)(2,1)S(1)} %bitcast.113), kind=kOutput, calls=%fused_computation.16 | convolution fusion | flops 3222798336 | bytes 10485760 | tf_op jit(solution)/shard_map/prf,fqd->pqrd/dot_general | solution.py:68
  97.5 0.0 slice-done.4
  97.5 6.8 %add_convert_fusion = bf16[2,256,3072]{2,1,0:T(8,128)(2,1)} fusion(f32[2,256,3072]{2,1,0:T(8,128)} %fusion, bf16[2,256,1024]{2,1,0:T(8,128)(2,1)S(1)} %bitcast.122, bf16[1,3072,1024]{2,1,0:T(8,128)(2,1)S(1)} %bitcast.115), kind=kOutput, calls=%fused_computation.15 | convolution fusion | flops 3224371200 | bytes 16777216 | tf_op jit(solution)/shard_map/prf,qdf->pqrd/dot_general | solution.py:105
  104.3 0.0 all-reduce.3.cloned.1.call-update
  104.4 137.3 %all-reduce.3.cloned.1.call-done = (bf16[2,256,3072]{2,1,0:T(8,128)(2,1)}, bf16[2,256,3072]{2,1,0:T(8,128)(2,1)}) async-done(((bf16[2,256,3072]{2,1,0:T(8,128)(2,1)}, bf16[2,256,3072]{2,1,0:T(8,128)(2,1)}), (bf16[2,256,3072]{2,1,0:T(8,128)(2,1)}, bf16[2,256,3072]{2,1,0:T(8,128)(2,1)})) %all-reduce.3.cloned.1.call-update) | async-done | bytes 6291472 | tf_op jit(solution)/shard_map/psum | solution.py:51
  241.6 2.7 convert_convert_fusion
  244.3 3.7 %all-to-all-start.3 = ((bf16[4,64,3072]{2,1,0:T(8,128)(2,1)}), bf16[4,64,3072]{2,1,0:T(8,128)(2,1)S(1)}, u32[]{:S(2)}, u32[]{:S(2)}) async-start(bf16[4,64,3072]{2,1,0:T(8,128)(2,1)} %bitcast.107), calls=%async_computation.3 | async-start | bytes 3145728 | tf_op jit(solution)/shard_map/all_to_all | solution.py:56
  248.1 0.0 copy-done.4
  248.1 8.5 %convert_bitcast_fusion = bf16[1,1024,3072]{2,1,0:T(8,128)(2,1)} fusion(bf16[512,1024]{1,0:T(8,128)(2,1)} %copy-done.10, bf16[512,3072]{1,0:T(8,128)(2,1)} %bitcast.121), kind=kOutput, calls=%fused_computation.12 | convolution fusion | flops 3224371200 | bytes 10485760 | tf_op jit(solution)/shard_map/rf,rd->fd/dot_general | solution.py:94
  256.6 1.3 convert_convert_fusion.1
  257.9 8.6 %all-to-all-done.3 = bf16[4,64,3072]{2,1,0:T(8,128)(2,1)S(1)} async-done(((bf16[4,64,3072]{2,1,0:T(8,128)(2,1)}), bf16[4,64,3072]{2,1,0:T(8,128)(2,1)S(1)}, u32[]{:S(2)}, u32[]{:S(2)}) %all-to-all-start.3) | async-done | bytes 1572896 | tf_op jit(solution)/shard_map/all_to_all | solution.py:56
  266.6 4.4 %all-to-all-start.1 = ((bf16[4,64,3072]{2,1,0:T(8,128)(2,1)}), bf16[4,64,3072]{2,1,0:T(8,128)(2,1)}, u32[]{:S(2)}, u32[]{:S(2)}) async-start(bf16[4,64,3072]{2,1,0:T(8,128)(2,1)} %bitcast.106), calls=%async_computation.1 | async-start | bytes 3145728 | tf_op jit(solution)/shard_map/all_to_all | solution.py:56
  270.9 8.5 %convert_bitcast_fusion.1 = bf16[1,3072,1024]{2,1,0:T(8,128)(2,1)} fusion(bf16[512,3072]{1,0:T(8,128)(2,1)} %bitcast.117, bf16[512,1024]{1,0:T(8,128)(2,1)} %copy-done.9), kind=kOutput, calls=%fused_computation.13 | convolution fusion | flops 3224371200 | bytes 10485760 | tf_op jit(solution)/shard_map/rd,rf->df/dot_general | solution.py:100
  279.5 5.4 %convert_bitcast_fusion.2 = bf16[1,3072,1024]{2,1,0:T(8,128)(2,1)} fusion(bf16[512,3072]{1,0:T(8,128)(2,1)S(1)} %bitcast.119, bf16[512,1024]{1,0:T(8,128)(2,1)S(1)} %copy-done.8), kind=kOutput, calls=%fused_computation.14 | convolution fusion | flops 3224371200 | bytes 10485760 | tf_op jit(solution)/shard_map/rd,rf->df/dot_general | solution.py:97
  284.8 1.6 fusion.28
  286.4 3.3 all-to-all-done.1
  289.7 2.1 multiply_reduce_fusion
  291.8 0.3 fusion.20
  292.0 1.6 fusion.19
  293.7 28.0 %psum.23 = bf16[3072,4]{0,1:T(4,128)(2,1)S(1)} all-reduce(bf16[3072,4]{0,1:T(4,128)(2,1)S(1)} %fusion.20), channel_id=1, replica_groups=mesh['dp'=2,'expert'=4,'mp'=4] {'dp','expert'}, use_global_device_ids=true, to_apply=%region_8.9 | all-reduce | flops 12288 | bytes 49152 | tf_op jit(solution)/shard_map/psum | solution.py:86
  321.7 0.6 convert_element_type.116
  322.3 0.9 fusion.24
  (26 shorter events, 0.1 us)
Async XLA Ops:
  7.2 1.0 copy-start
  7.2 50.8 %all-gather.5.cloned.1.call-start = ((), (), s32[]{:S(2)}) async-start(), calls=%async_computation.5 | async-start | bytes 4718592 | tf_op jit(solution)/shard_map/all_gather | solution.py:45
  36.9 36.4 %all-gather.3.cloned.1.call-start = ((), (), s32[]{:S(2)}) async-start(), calls=%async_computation.4 | async-start | bytes 4718592 | tf_op jit(solution)/shard_map/all_gather | solution.py:45
  57.9 183.7 %all-reduce.3.cloned.1.call-start = ((), (), s32[]{:S(2)}) async-start(), calls=%async_computation.6 | async-start | bytes 12582912 | tf_op jit(solution)/shard_map/psum | solution.py:51
  73.3 6.6 %copy-start.5 = (bf16[8,64,3072]{2,1,0:T(8,128)(2,1)S(1)}, bf16[8,64,3072]{2,1,0:T(8,128)(2,1)}, u32[]{:S(2)}) copy-start(bf16[8,64,3072]{2,1,0:T(8,128)(2,1)} %all-gather.3.cloned.1.call-done) | copy-start | bytes 9437188
  73.3 14.0 %slice-start = ((s8[6291456]{0:T(1024)(128)(4,1)}), s8[4194304]{0:T(1024)(128)(4,1)S(1)}, s32[]{:S(2)}) async-start(s8[6291456]{0:T(1024)(128)(4,1)} %bitcast.110), calls=%async_computation.7 | async-start | bytes 8388608
  73.3 19.4 %slice-start.2 = ((s8[6291456]{0:T(1024)(128)(4,1)}), s8[4194304]{0:T(1024)(128)(4,1)S(1)}, s32[]{:S(2)}) async-start(s8[6291456]{0:T(1024)(128)(4,1)} %bitcast.112), calls=%async_computation.9 | async-start | bytes 8388608
  79.9 7.4 %slice-start.1 = ((s8[6291456]{0:T(1024)(128)(4,1)}), s8[2097152]{0:T(1024)(128)(4,1)S(1)}, s32[]{:S(2)}) async-start(s8[6291456]{0:T(1024)(128)(4,1)} %bitcast.110), calls=%async_computation.8 | async-start | bytes 4194304
  79.9 12.8 %slice-start.3 = ((s8[6291456]{0:T(1024)(128)(4,1)}), s8[2097152]{0:T(1024)(128)(4,1)S(1)}, s32[]{:S(2)}) async-start(s8[6291456]{0:T(1024)(128)(4,1)} %bitcast.112), calls=%async_computation.10 | async-start | bytes 4194304
  79.9 17.6 %slice-start.4 = ((s8[6291456]{0:T(1024)(128)(4,1)}), s8[4194304]{0:T(1024)(128)(4,1)S(1)}, s32[]{:S(2)}) async-start(s8[6291456]{0:T(1024)(128)(4,1)} %bitcast.114), calls=%async_computation.11 | async-start | bytes 8388608
  87.2 5.4 %copy-start.9 = (bf16[512,1024]{1,0:T(8,128)(2,1)}, bf16[512,1024]{1,0:T(8,128)(2,1)S(1)}, u32[]{:S(2)}) copy-start(bf16[512,1024]{1,0:T(8,128)(2,1)S(1)} %get-tuple-element.11) | copy-start | bytes 3145732
  87.2 5.4 %copy-start.10 = (bf16[512,1024]{1,0:T(8,128)(2,1)}, bf16[512,1024]{1,0:T(8,128)(2,1)S(1)}, u32[]{:S(2)}) copy-start(bf16[512,1024]{1,0:T(8,128)(2,1)S(1)} %get-tuple-element.12) | copy-start | bytes 3145732
  87.2 10.3 %copy-start.7 = (bf16[512,1024]{1,0:T(8,128)(2,1)}, bf16[512,1024]{1,0:T(8,128)(2,1)S(1)}, u32[]{:S(2)}) copy-start(bf16[512,1024]{1,0:T(8,128)(2,1)S(1)} %get-tuple-element.10) | copy-start | bytes 3145732
  87.3 10.2 %slice-start.5 = ((s8[6291456]{0:T(1024)(128)(4,1)}), s8[2097152]{0:T(1024)(128)(4,1)S(1)}, s32[]{:S(2)}) async-start(s8[6291456]{0:T(1024)(128)(4,1)} %bitcast.114), calls=%async_computation.12 | async-start | bytes 4194304
  241.6 6.4 %copy-start.4 = (s32[64,2]{0,1:T(2,128)S(1)}, s32[64,2]{0,1:T(2,128)}, u32[]{:S(2)}) copy-start(s32[64,2]{0,1:T(2,128)} %param.10) | copy-start | bytes 1540
  244.3 22.3 %all-to-all-start.3 = ((bf16[4,64,3072]{2,1,0:T(8,128)(2,1)}), bf16[4,64,3072]{2,1,0:T(8,128)(2,1)S(1)}, u32[]{:S(2)}, u32[]{:S(2)}) async-start(bf16[4,64,3072]{2,1,0:T(8,128)(2,1)} %bitcast.107), calls=%async_computation.3 | async-start | bytes 3145728 | tf_op jit(solution)/shard_map/all_to_all | solution.py:56
  248.1 8.6 %copy-start.2 = (bf16[2,256,3072]{2,1,0:T(8,128)(2,1)S(1)}, bf16[2,256,3072]{2,1,0:T(8,128)(2,1)}, u32[]{:S(2)}) copy-start(bf16[2,256,3072]{2,1,0:T(8,128)(2,1)} %get-tuple-element.6) | copy-start | bytes 9437188
  266.6 23.1 %all-to-all-start.1 = ((bf16[4,64,3072]{2,1,0:T(8,128)(2,1)}), bf16[4,64,3072]{2,1,0:T(8,128)(2,1)}, u32[]{:S(2)}, u32[]{:S(2)}) async-start(bf16[4,64,3072]{2,1,0:T(8,128)(2,1)} %bitcast.106), calls=%async_computation.1 | async-start | bytes 3145728 | tf_op jit(solution)/shard_map/all_to_all | solution.py:56
  270.9 8.5 %copy-start.6 = (bf16[8,64,3072]{2,1,0:T(8,128)(2,1)S(1)}, bf16[8,64,3072]{2,1,0:T(8,128)(2,1)}, u32[]{:S(2)}) copy-start(bf16[8,64,3072]{2,1,0:T(8,128)(2,1)} %all-gather.3.cloned.1.call-done) | copy-start | bytes 9437188
  270.9 8.5 %copy-start.8 = (bf16[512,1024]{1,0:T(8,128)(2,1)S(1)}, bf16[512,1024]{1,0:T(8,128)(2,1)}, u32[]{:S(2)}) copy-start(bf16[512,1024]{1,0:T(8,128)(2,1)} %copy-done.7) | copy-start | bytes 3145732
  284.8 7.2 %copy-start.3 = (f32[3072,4]{0,1:T(4,128)S(1)}, f32[3072,4]{0,1:T(4,128)}, u32[]{:S(2)}) copy-start(f32[3072,4]{0,1:T(4,128)} %param.9) | copy-start | bytes 147460
  289.7 2.4 copy-start.1
Sparse Core Ops, SparseCore 0:
  37.0 13.7 all-gather.4
  58.1 15.1 all-gather.2
  104.5 137.1 all-reduce.2
where the time goes:
time: 330 us
  waiting for transfers between devices  158 us (48%)
  blocking collectives  71 us (22%)
  matrix products  67.8 us (21%)
  between operations  14.1 us (4%)
  other arithmetic  9.3 us (3%)
  starting transfers between devices  8.22 us (2%)
    psum x1, waiting for transfers between devices, combine(): lax.psum(partial_value.reshape(dp_count, block_rows, features).astype(jnp...  137 us
    all_to_all x2, blocking collectives, spread(): lax.all_to_all(buffer, 'expert', split_axis=0, concat_axis=0, tiled=True)  43 us
    psum x1, blocking collectives, local(): lax.psum(router_term.astype(jnp.bfloat16), ('dp', 'expert'))  28 us
    all_to_all x2, waiting for transfers between devices, combine(): lax.all_to_all(own_rows, 'expert', split_axis=0, concat_axis=0, tiled=True)  11.9 us
    all_gather x2, waiting for transfers between devices, spread(): return lax.all_gather(arrived, 'dp', axis=0, tiled=True)  8.71 us
    dot_general x1, matrix products, local(): jnp.einsum('rf,rd->fd', hidden, cot_in, preferred_element_type=jnp.float32)  8.54 us
    dot_general x1, matrix products, local(): jnp.einsum('rd,rf->df', rows_in, up_grad, preferred_element_type=jnp.floa...  8.5 us
    all_to_all x2, starting transfers between devices, combine(): lax.all_to_all(own_rows, 'expert', split_axis=0, concat_axis=0, tiled=True)  8.1 us
  transfers between devices with their start and end apart: 5, of which 4 were waited for; matrix products, arithmetic and copies ran while one was open for 10% of the time, Pallas kernels for 0%

commit v1 on v0

--- a/solution.py
+++ b/solution.py
@@ -48,8 +48,12 @@
     pieces = 1
 
     def combine(partial_value):
-        summed = lax.psum(
-            partial_value.reshape(dp_count, block_rows, features).astype(jnp.bfloat16), ("dp", "mp")
+        summed = jnp.sum(
+            lax.all_gather(
+                partial_value.reshape(dp_count, block_rows, features).astype(jnp.bfloat16),
+                axis_name=("dp", "mp"),
+            ),
+            axis=0,
         ).astype(jnp.float32)
         own_rows = lax.dynamic_index_in_dim(summed, lax.axis_index("dp"), 0, keepdims=False)
         own_rows = own_rows.astype(jnp.bfloat16).reshape(exp_count, slot_count, features)

time: 330 us -> 657 us (1.99)
  waiting for transfers between devices: 158 us -> 454 us
  other arithmetic: 9.3 us -> 34.4 us
    all_gather x0 -> x2, waiting for transfers between devices: none -> 406 us  [combine(): lax.all_gather(partial_value.reshape(dp_count, block_rows, features).asty...]
    psum x1 -> x0, waiting for transfers between devices: 137 us -> none  [combine(): lax.psum(partial_value.reshape(dp_count, block_rows, features).astype(jnp...]
    reduce_sum x0 -> x2, other arithmetic: none -> 28.2 us  [combine(): jnp.sum(lax.all_gather(partial_value.reshape(dp_count, block_rows, featur...]
    all_gather x2, waiting for transfers between devices: 8.71 us -> 24.9 us  [spread(): return lax.all_gather(arrived, 'dp', axis=0, tiled=True)]
    all_to_all x2, waiting for transfers between devices: 11.9 us -> 23.3 us  [combine(): lax.all_to_all(own_rows, 'expert', split_axis=0, concat_axis=0, tiled=True)]
  transfers between devices with their start and end apart: 5 -> 6, of which waited for: 4 -> 6; matrix products, arithmetic and copies ran while one was open for 10% -> 4% of each run, Pallas kernels for 0% -> 0%
where the time goes in v1:
time: 657 us; the launch traced here: 655 us
  waiting for transfers between devices  454 us (69%)
  blocking collectives  71.6 us (11%)
  matrix products  70.4 us (11%)
  other arithmetic  34.4 us (5%)
  between operations  14 us (2%)
  starting transfers between devices  7.82 us (1%)
    all_gather x2, waiting for transfers between devices, combine(): lax.all_gather(partial_value.reshape(dp_count, block_rows, features).asty...  406 us
    all_to_all x2, blocking collectives, spread(): lax.all_to_all(buffer, 'expert', split_axis=0, concat_axis=0, tiled=True)  44.1 us
    reduce_sum x2, other arithmetic, combine(): jnp.sum(lax.all_gather(partial_value.reshape(dp_count, block_rows, featur...  28.2 us
    psum x1, blocking collectives, local(): lax.psum(router_term.astype(jnp.bfloat16), ('dp', 'expert'))  27.5 us
    all_gather x2, waiting for transfers between devices, spread(): return lax.all_gather(arrived, 'dp', axis=0, tiled=True)  24.9 us
    all_to_all x2, waiting for transfers between devices, combine(): lax.all_to_all(own_rows, 'expert', split_axis=0, concat_axis=0, tiled=True)  23.3 us
  transfers between devices with their start and end apart: 6, of which 6 were waited for; matrix products, arithmetic and copies ran while one was open for 4% of the time, Pallas kernels for 0%

profile of v1, /device:TPU:1, one launch (start us, length us, event | category | flops | bytes accessed | tf_op | source)
XLA Modules:
  0.0 654.8 jit_solution(16385268863489094375)
XLA Ops:
  7.2 0.0 copy-start
  7.2 0.0 all-gather.7.cloned.1.call-start
  7.2 0.8 copy.31
  8.0 0.1 eq.38
  8.2 0.1 fusion.40
  8.3 0.2 reduce_window_sum.11
  8.4 0.2 select_reduce_fusion
  8.6 0.1 reshape.93
  8.8 0.1 copy.32
  8.8 0.8 select_reduce_fusion.1
  9.6 0.7 fusion.44
  10.3 0.1 convert_reduce_fusion
  10.4 0.0 copy-done
  10.4 0.6 fusion.49
  11.0 22.7 %all_to_all.20 = bf16[4,64,3072]{2,1,0:T(8,128)(2,1)} all-to-all(bf16[4,64,3072]{2,1,0:T(8,128)(2,1)S(1)} %bitcast.136), channel_id=1, replica_groups=mesh['dp'=2,'expert'=4,'mp'=4] {'expert'}, dimensions={0} | all-to-all | bytes 3145728 | tf_op jit(solution)/shard_map/all_to_all | solution.py:44
  33.7 0.0 all-gather.7.cloned.1.call-update
  33.7 0.0 all-gather.11.cloned.1.call-start
  33.7 13.9 %all-gather.7.cloned.1.call-done = bf16[8,64,3072]{2,1,0:T(8,128)(2,1)} async-done(((bf16[4,64,3072]{2,1,0:T(8,128)(2,1)}), bf16[8,64,3072]{2,1,0:T(8,128)(2,1)}) %all-gather.7.cloned.1.call-update) | async-done | bytes 3145744 | tf_op jit(solution)/shard_map/all_gather | solution.py:45
  47.6 7.4 %fusion.10 = f32[512,1024]{1,0:T(8,128)S(1)} fusion(bf16[512,3072]{1,0:T(8,128)(2,1)} %bitcast.143, bf16[1,3072,1024]{2,1,0:T(8,128)(2,1)} %param.12), kind=kOutput, calls=%fused_computation.12 | convolution fusion | flops 3221225472 | bytes 11534336 | tf_op jit(solution)/shard_map/dot_general | solution.py:66
  55.0 0.0 copy-done.6
  55.0 0.0 copy-start.13
  55.1 8.3 %multiply_convert_fusion.2 = (bf16[512,1024]{1,0:T(8,128)(2,1)S(1)}, f32[512,1024]{1,0:T(8,128)}) fusion(f32[512,1024]{1,0:T(8,128)S(1)} %fusion.10, bf16[512,3072]{1,0:T(8,128)(2,1)S(1)} %bitcast.146, bf16[1,3072,1024]{2,1,0:T(8,128)(2,1)} %param.13), kind=kOutput, calls=%fused_computation.33 | convolution fusion | flops 3224371200 | bytes 14680064 | tf_op jit(solution)/shard_map/dot_general | solution.py:67
  63.4 0.0 copy-done.13
  63.4 0.0 slice-done
  63.4 0.0 slice-done.1
  63.4 4.8 fusion.17
  68.2 0.0 copy-done.8
  68.2 0.0 all-gather.11.cloned.1.call-update
  68.2 221.2 %all-gather.11.cloned.1.call-done = bf16[16,1,256,3072]{3,2,1,0:T(8,128)(2,1)} async-done(((bf16[2,1,256,3072]{3,2,1,0:T(8,128)(2,1)}), bf16[16,1,256,3072]{3,2,1,0:T(8,128)(2,1)}) %all-gather.11.cloned.1.call-update) | async-done | bytes 25165840 | tf_op jit(solution)/shard_map/all_gather | solution.py:52
  289.5 14.1 %bitcast_reduce_fusion.1 = bf16[2,256,3072]{2,1,0:T(8,128)(2,1)S(1)} fusion(bf16[8,2,256,3072]{3,2,1,0:T(8,128)(2,1)} %bitcast.132), kind=kLoop, calls=%fused_computation.1 | loop fusion | flops 11010048 | bytes 28311552 | tf_op jit(solution)/shard_map/reduce_sum | solution.py:51
  303.6 1.3 convert_convert_fusion.1
  304.8 3.7 all-to-all-start.1
  308.5 0.0 all-gather.9.cloned.1.call-start
  308.6 0.0 copy-done.2
  308.6 0.1 convert_element_type.146
  308.7 0.4 fusion.48
  309.1 0.0 copy-done.5
  309.1 18.4 %all-to-all-done.1 = bf16[4,64,3072]{2,1,0:T(8,128)(2,1)S(1)} async-done(((bf16[4,64,3072]{2,1,0:T(8,128)(2,1)}), bf16[4,64,3072]{2,1,0:T(8,128)(2,1)S(1)}, u32[]{:S(2)}, u32[]{:S(2)}) %all-to-all-start.1) | async-done | bytes 1572896 | tf_op jit(solution)/shard_map/all_to_all | solution.py:60
  327.5 1.1 copy-done.1
  328.7 1.9 multiply_reduce_fusion
  330.6 0.7 fusion.23
  331.3 21.4 %all_to_all.21 = bf16[4,64,3072]{2,1,0:T(8,128)(2,1)} all-to-all(bf16[4,64,3072]{2,1,0:T(8,128)(2,1)S(1)} %bitcast.139), channel_id=1, replica_groups=mesh['dp'=2,'expert'=4,'mp'=4] {'expert'}, dimensions={0} | all-to-all | bytes 3145728 | tf_op jit(solution)/shard_map/all_to_all | solution.py:44
  352.7 0.0 all-gather.9.cloned.1.call-update
  352.8 0.2 all-gather.13.cloned.1.call-start
  353.0 11.0 %all-gather.9.cloned.1.call-done = bf16[8,64,3072]{2,1,0:T(8,128)(2,1)} async-done(((bf16[4,64,3072]{2,1,0:T(8,128)(2,1)}), bf16[8,64,3072]{2,1,0:T(8,128)(2,1)}) %all-gather.9.cloned.1.call-update) | async-done | bytes 3145744 | tf_op jit(solution)/shard_map/all_gather | solution.py:45
  364.0 8.9 %multiply_convert_fusion.1 = (bf16[512,1024]{1,0:T(8,128)(2,1)S(1)}, bf16[512,1024]{1,0:T(8,128)(2,1)S(1)}) fusion(f32[512,1024]{1,0:T(8,128)} %copy-done.13, f32[512,1024]{1,0:T(8,128)} %get-tuple-element.13, bf16[512,3072]{1,0:T(8,128)(2,1)} %bitcast.147, bf16[1,1024,3072]{2,1,0:T(8,128)(2,1)} %param.14), kind=kOutput, calls=%fused_computation.32 | convolution fusion | flops 3228041216 | bytes 15728640 | tf_op jit(solution)/shard_map/rd,fd->rf/dot_general | solution.py:93
  372.9 0.0 copy-start.11
  372.9 6.3 fusion
  379.3 7.7 %fusion.20 = bf16[2,1,256,3072]{3,2,1,0:T(8,128)(2,1)} fusion(f32[2,256,3072]{2,1,0:T(8,128)S(1)} %fusion, bf16[2,256,1024]{2,1,0:T(8,128)(2,1)S(1)} %bitcast.151, bf16[1,3072,1024]{2,1,0:T(8,128)(2,1)} %param.12), kind=kOutput, calls=%fused_computation.20 | convolution fusion | flops 3224371200 | bytes 16777216 | tf_op jit(solution)/shard_map/prf,qdf->pqrd/dot_general | solution.py:109
  387.0 0.0 all-gather.13.cloned.1.call-update
  387.0 0.3 fusion.26
  387.3 27.5 %psum.7 = bf16[3072,4]{0,1:T(4,128)(2,1)S(1)} all-reduce(bf16[3072,4]{0,1:T(4,128)(2,1)S(1)} %fusion.26), channel_id=1, replica_groups=mesh['dp'=2,'expert'=4,'mp'=4] {'dp','expert'}, use_global_device_ids=true, to_apply=%region_8.9 | all-reduce | flops 12288 | bytes 49152 | tf_op jit(solution)/shard_map/psum | solution.py:90
  414.8 0.6 convert_element_type.162
  415.5 0.9 fusion.30
  416.4 7.2 %convert_bitcast_fusion.2 = bf16[1,3072,1024]{2,1,0:T(8,128)(2,1)} fusion(bf16[512,3072]{1,0:T(8,128)(2,1)} %bitcast.144, bf16[512,1024]{1,0:T(8,128)(2,1)S(1)} %copy-done.12), kind=kOutput, calls=%fused_computation.16 | convolution fusion | flops 3224371200 | bytes 10485760 | tf_op jit(solution)/shard_map/rd,rf->df/dot_general | solution.py:101
  423.6 184.6 %all-gather.13.cloned.1.call-done = bf16[16,1,256,3072]{3,2,1,0:T(8,128)(2,1)} async-done(((bf16[2,1,256,3072]{3,2,1,0:T(8,128)(2,1)}), bf16[16,1,256,3072]{3,2,1,0:T(8,128)(2,1)}) %all-gather.13.cloned.1.call-update) | async-done | bytes 25165840 | tf_op jit(solution)/shard_map/all_gather | solution.py:52
  608.3 14.1 %bitcast_reduce_fusion = bf16[2,256,3072]{2,1,0:T(8,128)(2,1)S(1)} fusion(bf16[8,2,256,3072]{3,2,1,0:T(8,128)(2,1)} %bitcast.133), kind=kLoop, calls=%fused_computation | loop fusion | flops 11010048 | bytes 28311552 | tf_op jit(solution)/shard_map/reduce_sum | solution.py:51
  622.4 1.3 convert_convert_fusion
  623.7 3.8 all-to-all-start.3
  627.5 8.5 %convert_bitcast_fusion.1 = bf16[1,3072,1024]{2,1,0:T(8,128)(2,1)} fusion(bf16[512,3072]{1,0:T(8,128)(2,1)} %bitcast.145, bf16[512,1024]{1,0:T(8,128)(2,1)} %copy-done.10), kind=kOutput, calls=%fused_computation.15 | convolution fusion | flops 3224371200 | bytes 10485760 | tf_op jit(solution)/shard_map/rd,rf->df/dot_general | solution.py:104
  636.0 5.4 convert_bitcast_fusion
  641.3 4.9 all-to-all-done.3
  646.2 0.4 fusion.34
  646.6 1.6 fusion.25
  (26 shorter events, 0.1 us)
Async XLA Ops:
  7.2 3.2 copy-start
  7.2 40.4 %all-gather.7.cloned.1.call-start = ((), (), s32[]{:S(2)}) async-start(), calls=%async_computation.4 | async-start | bytes 4718592 | tf_op jit(solution)/shard_map/all_gather | solution.py:45
  33.7 29.7 %slice-start = ((s8[6291456]{0:T(1024)(128)(4,1)}), s8[2097152]{0:T(1024)(128)(4,1)S(1)}, s32[]{:S(2)}) async-start(s8[6291456]{0:T(1024)(128)(4,1)} %bitcast.141), calls=%async_computation.8 | async-start | bytes 4194304
  33.7 255.8 %all-gather.11.cloned.1.call-start = ((), (), s32[]{:S(2)}) async-start(), calls=%async_computation.6 | async-start | bytes 28311552 | tf_op jit(solution)/shard_map/all_gather | solution.py:52
  47.6 7.4 %copy-start.6 = (bf16[8,64,3072]{2,1,0:T(8,128)(2,1)S(1)}, bf16[8,64,3072]{2,1,0:T(8,128)(2,1)}, u32[]{:S(2)}) copy-start(bf16[8,64,3072]{2,1,0:T(8,128)(2,1)} %all-gather.7.cloned.1.call-done) | copy-start | bytes 9437188
  47.6 15.8 %slice-start.1 = ((s8[6291456]{0:T(1024)(128)(4,1)}), s8[4194304]{0:T(1024)(128)(4,1)S(1)}, s32[]{:S(2)}) async-start(s8[6291456]{0:T(1024)(128)(4,1)} %bitcast.141), calls=%async_computation.9 | async-start | bytes 8388608
  55.0 8.3 %copy-start.13 = (f32[512,1024]{1,0:T(8,128)}, f32[512,1024]{1,0:T(8,128)S(1)}, u32[]{:S(2)}) copy-start(f32[512,1024]{1,0:T(8,128)S(1)} %fusion.10) | copy-start | bytes 6291460
  63.4 4.8 copy-start.8
  304.8 3.8 copy-start.2
  304.8 3.8 copy-start.3
  304.8 4.2 copy-start.5
  304.8 22.7 %all-to-all-start.1 = ((bf16[4,64,3072]{2,1,0:T(8,128)(2,1)}), bf16[4,64,3072]{2,1,0:T(8,128)(2,1)S(1)}, u32[]{:S(2)}, u32[]{:S(2)}) async-start(bf16[4,64,3072]{2,1,0:T(8,128)(2,1)} %bitcast.138), calls=%async_computation.1 | async-start | bytes 3145728 | tf_op jit(solution)/shard_map/all_to_all | solution.py:60
  308.5 55.5 %all-gather.9.cloned.1.call-start = ((), (), s32[]{:S(2)}) async-start(), calls=%async_computation.5 | async-start | bytes 4718592 | tf_op jit(solution)/shard_map/all_gather | solution.py:45
  327.5 1.1 copy-start.1
  352.8 255.5 %all-gather.13.cloned.1.call-start = ((), (), s32[]{:S(2)}) async-start(), calls=%async_computation.7 | async-start | bytes 28311552 | tf_op jit(solution)/shard_map/all_gather | solution.py:52
  372.9 6.4 copy-start.10
  372.9 6.4 copy-start.11
  387.0 29.4 %copy-start.12 = (bf16[512,1024]{1,0:T(8,128)(2,1)S(1)}, bf16[512,1024]{1,0:T(8,128)(2,1)}, u32[]{:S(2)}) copy-start(bf16[512,1024]{1,0:T(8,128)(2,1)} %copy-done.11) | copy-start | bytes 3145732
  623.7 22.5 %all-to-all-start.3 = ((bf16[4,64,3072]{2,1,0:T(8,128)(2,1)}), bf16[4,64,3072]{2,1,0:T(8,128)(2,1)S(1)}, u32[]{:S(2)}, u32[]{:S(2)}) async-start(bf16[4,64,3072]{2,1,0:T(8,128)(2,1)} %bitcast.137), calls=%async_computation.3 | async-start | bytes 3145728 | tf_op jit(solution)/shard_map/all_to_all | solution.py:60
  627.5 8.5 %copy-start.7 = (bf16[8,64,3072]{2,1,0:T(8,128)(2,1)S(1)}, bf16[8,64,3072]{2,1,0:T(8,128)(2,1)}, u32[]{:S(2)}) copy-start(bf16[8,64,3072]{2,1,0:T(8,128)(2,1)} %all-gather.9.cloned.1.call-done) | copy-start | bytes 9437188
  627.5 8.5 %copy-start.9 = (bf16[512,1024]{1,0:T(8,128)(2,1)S(1)}, bf16[512,1024]{1,0:T(8,128)(2,1)}, u32[]{:S(2)}) copy-start(bf16[512,1024]{1,0:T(8,128)(2,1)} %copy-done.8) | copy-start | bytes 3145732
  641.3 5.3 copy-start.4
Sparse Core Ops, SparseCore 0:
  33.8 13.7 all-gather.6
  68.3 221.0 all-gather.10
  352.9 11.0 all-gather.8
  387.1 221.0 all-gather.12
